TPU v7x, 128 devices: a whole 4x4x4 slice. The times are simulated.
128 devices in a mesh: chi: 2 (over core), phi: 64 (over z, y, x).
Axes of the slice: x: 4, y: 4, z: 4, core: 2. Of those that a mesh axis runs over, the one named last changes fastest.
Arguments:
- frames: bfloat16 [1024, 8, 8, 2048], P('phi', 'chi'), may hold values from 0.25 to 8
- drift_rows: int32 [1024, 8], P('phi', 'chi'), may hold values from -2 to 2
- drift_cols: int32 [1024, 8], P('phi', 'chi'), may hold values from -24 to 24
- weight_index: int32 [1024, 8], P('phi', 'chi'), may hold values from 0 to 63
- blur_band: int32 [16384], P('chi'), may hold values from 0 to 3
Outputs:
- restored: float32 [1024, 8, 16384], P('phi', None, 'chi')
All inputs are finite; a program needn't handle non-finite values.
Results may differ from a plain program's by a relative error of at most 0.0003.
Values sent between devices are 32-bit elements; how exact they have to be, the bound alone decides.
A program may use at most 128 MiB of HBM per device.

v0:
```python
import jax
import jax.numpy as jnp
from jax import lax
from jax.sharding import PartitionSpec as P

ITERS = 3


def shifted(shard, axis, by):
    length = lax.axis_size(axis)
    pairs = [(i, i + by) for i in range(length) if 0 <= i + by < length]
    return lax.ppermute(shard, axis, pairs)


def shift_one(frame, row_drift, col_drift, table_index):
    padded = jnp.pad(frame.astype(jnp.float32), ((3, 3), (25, 25)))
    frac_y = (table_index // 8).astype(jnp.float32) / 8.0
    frac_x = (table_index % 8).astype(jnp.float32) / 8.0
    summed = jnp.zeros(frame.shape, jnp.float32)
    for a in range(2):
        for b in range(2):
            factor = (frac_y if a else 1.0 - frac_y) * (frac_x if b else 1.0 - frac_x)
            start_row = 3 - row_drift - a
            start_col = 25 - col_drift - b
            window = lax.dynamic_slice(padded, (start_row, start_col), frame.shape)
            summed = summed + factor * window
    return summed.reshape(-1)


def tap_weights(band_index):
    spread = 0.8 + 0.6 * band_index.astype(jnp.float32)
    offsets = jnp.arange(-4, 5).astype(jnp.float32)
    unnormed = jnp.exp(-offsets[:, None] ** 2 / (2.0 * spread[None, :] ** 2))
    return unnormed / jnp.sum(unnormed, axis=0, keepdims=True)


def phi_blur(field, weights):
    number = field.shape[1]
    padded = jnp.pad(field, ((0, 0), (4, 4), (0, 0)))
    phi_sum = jnp.zeros(field.shape, jnp.float32)
    for k in range(9):
        phi_sum = phi_sum + weights[k][None, None, :] * padded[:, k : k + number, :]
    return phi_sum


def chi_mix(own, below, above):
    before = jnp.concatenate([below, own[:-1]], axis=0)
    after = jnp.concatenate([own[1:], above], axis=0)
    return 0.25 * before + 0.5 * own + 0.25 * after


def body(frames, drift_rows, drift_cols, weight_index, blur_band):
    corrected = jax.vmap(jax.vmap(shift_one))(frames, drift_rows, drift_cols, weight_index)
    pixel_tiles = lax.all_to_all(corrected, "chi", split_axis=2, concat_axis=1, tiled=True)
    weights = tap_weights(blur_band)
    estimate = pixel_tiles + 0.1
    for iteration in range(ITERS):
        summed = phi_blur(estimate, weights)
        below = shifted(summed[-1:], "phi", 1)
        above = shifted(summed[:1], "phi", -1)
        blurred = chi_mix(summed, below, above)
        ratio = pixel_tiles / (blurred + 0.1)
        ratio_sum = phi_blur(ratio, weights)
        ratio_below = shifted(ratio_sum[-1:], "phi", 1)
        ratio_above = shifted(ratio_sum[:1], "phi", -1)
        estimate = estimate * chi_mix(ratio_sum, ratio_below, ratio_above)
    return estimate


def solution(mesh):
    return jax.shard_map(
        body,
        mesh=mesh,
        in_specs=(
            P("phi", "chi", None, None),
            P("phi", "chi"),
            P("phi", "chi"),
            P("phi", "chi"),
            P("chi"),
        ),
        out_specs=P("phi", None, "chi"),
        check_vma=False,
    )
```

profile of v0, /device:TPU:30, one launch (start us, length us, event | category | flops | bytes accessed | tf_op | source)
XLA Modules:
  0.0 1755.4 jit_solution(11334240100492443829)
XLA Ops:
  0.9 8.4 pad_convert_fusion
  11.9 306.2 %while.4 = (s32[]{:T(128)}, f32[16,4,14,2098]{3,2,1,0:T(8,128)}, s32[64,4]{0,1:T(4,128)S(1)}, f32[64,8,2048]{2,1,0:T(8,128)}, s32[]{:T(128)}) while((s32[]{:T(128)}, f32[16,4,14,2098]{3,2,1,0:T(8,128)}, s32[64,4]{0,1:T(4,128)S(1)}, f32[64,8,2048]{2,1,0:T(8,128)}, s32[]{:T(128)}) %tuple.108), condition=%wide.while_cond, body=%wide.while_body.sunk | while | flops 2 | bytes 133761 | solution.py:25
  318.0 6.1 gather.21
  326.8 306.4 %while.5 = (s32[]{:T(128)}, f32[16,4,14,2098]{3,2,1,0:T(8,128)}, s32[64,4]{0,1:T(4,128)S(1)}, f32[64,8,2048]{2,1,0:T(8,128)}, s32[]{:T(128)}) while((s32[]{:T(128)}, f32[16,4,14,2098]{3,2,1,0:T(8,128)}, s32[64,4]{0,1:T(4,128)S(1)}, f32[64,8,2048]{2,1,0:T(8,128)}, s32[]{:T(128)}) %tuple.111), condition=%wide.while_cond.1, body=%wide.while_body.1.sunk | while | flops 2 | bytes 133761 | solution.py:25
  642.0 306.8 %while.6 = (s32[]{:T(128)}, f32[16,4,14,2098]{3,2,1,0:T(8,128)}, s32[64,4]{0,1:T(4,128)S(1)}, f32[64,8,2048]{2,1,0:T(8,128)}, s32[]{:T(128)}) while((s32[]{:T(128)}, f32[16,4,14,2098]{3,2,1,0:T(8,128)}, s32[64,4]{0,1:T(4,128)S(1)}, f32[64,8,2048]{2,1,0:T(8,128)}, s32[]{:T(128)}) %tuple.112), condition=%wide.while_cond.2, body=%wide.while_body.2.sunk | while | flops 2 | bytes 133761 | solution.py:25
  957.5 303.8 %while.7 = (s32[]{:T(128)}, f32[16,4,14,2098]{3,2,1,0:T(8,128)}, s32[64,4]{0,1:T(4,128)S(1)}, f32[64,8,2048]{2,1,0:T(8,128)}, s32[]{:T(128)}) while((s32[]{:T(128)}, f32[16,4,14,2098]{3,2,1,0:T(8,128)}, s32[64,4]{0,1:T(4,128)S(1)}, f32[64,8,2048]{2,1,0:T(8,128)}, s32[]{:T(128)}) %tuple.113), condition=%wide.while_cond.3, body=%wide.while_body.3.sunk | while | flops 2 | bytes 133761 | solution.py:25
  1267.7 8.6 multiply_add_fusion
  1276.3 23.6 %copy.59 = f32[16,4,16384]{0,1,2:T(4,128)} copy(f32[16,4,16384]{2,1,0:T(4,128)} %multiply_add_fusion) | data formatting | bytes 8388608 | tf_op jit(solution)/shard_map/vmap(vmap())/add | solution.py:26
  1299.9 42.6 %reshape.139 = f32[2,1,524288]{2,1,0:T(1,128)} reshape(f32[16384,4,16]{2,1,0:T(4,128)} %bitcast.94) | data formatting | bytes 8388608
  1353.1 16.7 reduce
  1369.8 44.6 %reshape.140 = f32[16384,4,16]{2,1,0:T(4,128)} reshape(f32[2,524288]{1,0:T(2,128)} %reduce) | data formatting | bytes 8388608
  1414.5 25.1 %copy.60 = f32[16,2,4,8192]{3,2,1,0:T(4,128)} copy(f32[16,2,4,8192]{0,2,3,1:T(4,128)} %bitcast.95) | data formatting | bytes 8388608 | tf_op jit(solution)/shard_map/all_to_all | solution.py:54
  1463.0 7.3 collective-permute-done.1
  1470.3 21.8 %fusion.99 = f32[16,8,8192]{2,1,0:T(8,128)} fusion(f32[16,8,8192]{2,1,0:T(8,128)} %all_to_all.16, f32[15,8,8192]{2,1,0:T(8,128)} %get-tuple-element.108, f32[1,8,8192]{2,1,0:T(8,128)S(1)} %collective-permute-done, f32[1,8,8192]{2,1,0:T(8,128)S(1)} %collective-permute-done.1, f32[15,8,8192]{2,1,0:T(8,128)} %get-tuple-element.107, f32[8192]{0:T(1024)S(1)} %bitcast.109, ...), kind=kLoop, calls=%fused_computation.157 | loop fusion | flops 27262976 | bytes 21266432 | tf_op jit(solution)/shard_map/div | solution.py:62
  1492.2 16.1 fusion.24
  1523.6 21.3 %fusion.102 = f32[16,8,8192]{2,1,0:T(8,128)} fusion(f32[15,8,8192]{2,1,0:T(8,128)} %get-tuple-element.104, f32[1,8,8192]{2,1,0:T(8,128)S(1)} %collective-permute-done.2, f32[1,8,8192]{2,1,0:T(8,128)S(1)} %collective-permute-done.3, f32[15,8,8192]{2,1,0:T(8,128)} %get-tuple-element.103, f32[16,8,8192]{2,1,0:T(8,128)} %all_to_all.16, f32[8192]{0:T(1024)S(1)} %bitcast.111, ...), kind=kLoop, calls=%fused_computation.162 | loop fusion | flops 27262976 | bytes 21266432 | tf_op jit(solution)/shard_map/mul | solution.py:66
  1544.9 16.6 fusion.40
  1576.0 21.8 %fusion.106 = f32[16,8,8192]{2,1,0:T(8,128)} fusion(f32[16,8,8192]{2,1,0:T(8,128)} %all_to_all.16, f32[15,8,8192]{2,1,0:T(8,128)} %get-tuple-element.100, f32[1,8,8192]{2,1,0:T(8,128)S(1)} %collective-permute-done.4, f32[1,8,8192]{2,1,0:T(8,128)S(1)} %collective-permute-done.5, f32[15,8,8192]{2,1,0:T(8,128)} %get-tuple-element.99, f32[8192]{0:T(1024)S(1)} %bitcast.113, ...), kind=kLoop, calls=%fused_computation.168 | loop fusion | flops 27262976 | bytes 21266432 | tf_op jit(solution)/shard_map/div | solution.py:62
  1597.8 16.1 fusion.56
  1628.4 21.3 %fusion.109 = f32[16,8,8192]{2,1,0:T(8,128)} fusion(f32[16,8,8192]{2,1,0:T(8,128)} %fusion.102, f32[15,8,8192]{2,1,0:T(8,128)} %get-tuple-element.96, f32[1,8,8192]{2,1,0:T(8,128)S(1)} %collective-permute-done.6, f32[1,8,8192]{2,1,0:T(8,128)S(1)} %collective-permute-done.7, f32[15,8,8192]{2,1,0:T(8,128)} %get-tuple-element.95, f32[8192]{0:T(1024)S(1)} %bitcast.115, ...), kind=kLoop, calls=%fused_computation.173 | loop fusion | flops 26214400 | bytes 21266432 | tf_op jit(solution)/shard_map/mul | solution.py:66
  1649.7 16.6 fusion.72
  1680.8 21.8 %fusion.113 = f32[16,8,8192]{2,1,0:T(8,128)} fusion(f32[16,8,8192]{2,1,0:T(8,128)} %all_to_all.16, f32[15,8,8192]{2,1,0:T(8,128)} %get-tuple-element.92, f32[1,8,8192]{2,1,0:T(8,128)S(1)} %collective-permute-done.8, f32[1,8,8192]{2,1,0:T(8,128)S(1)} %collective-permute-done.9, f32[15,8,8192]{2,1,0:T(8,128)} %get-tuple-element.91, f32[8192]{0:T(1024)S(1)} %bitcast.117, ...), kind=kLoop, calls=%fused_computation.179 | loop fusion | flops 27262976 | bytes 21266432 | tf_op jit(solution)/shard_map/div | solution.py:62
  1702.6 16.3 fusion.88
  1733.4 21.5 %fusion.116 = f32[16,8,8192]{2,1,0:T(8,128)} fusion(f32[16,8,8192]{2,1,0:T(8,128)} %fusion.109, f32[15,8,8192]{2,1,0:T(8,128)} %get-tuple-element.88, f32[1,8,8192]{2,1,0:T(8,128)S(1)} %collective-permute-done.10, f32[1,8,8192]{2,1,0:T(8,128)S(1)} %collective-permute-done.11, f32[15,8,8192]{2,1,0:T(8,128)} %get-tuple-element.87, f32[8192]{0:T(1024)S(1)} %bitcast.119, ...), kind=kLoop, calls=%fused_computation.184 | loop fusion | flops 26214400 | bytes 21266432 | tf_op jit(solution)/shard_map/mul | solution.py:66
  (845 shorter events, 1359.8 us)
Async XLA Ops:
  1261.3 6.0 copy-start.2
  1342.5 10.1 all-to-all-start
  1444.8 2.6 copy-start.1
  1447.4 5.3 copy-start
  1452.8 10.2 collective-permute-start
  1456.2 14.2 collective-permute-start.1
  1508.4 10.0 collective-permute-start.2
  1510.3 13.3 collective-permute-start.3
  1561.6 10.0 collective-permute-start.4
  1563.5 12.5 collective-permute-start.5
  1614.0 10.1 collective-permute-start.6
  1615.9 12.5 collective-permute-start.7
  1666.4 10.2 collective-permute-start.8
  1668.3 12.5 collective-permute-start.9
  1719.0 9.9 collective-permute-start.10
  1720.9 12.5 collective-permute-start.11
where the time goes:
time: 1780 us; the launch traced here: 1760 us
  local copies, waits for them, and re-layouts  1420 us (80%)
  other arithmetic  254 us (14%)
  starting transfers between devices  41.6 us (2%)
  waiting for transfers between devices  35.1 us (2%)
    gather x768, local copies, waits for them, and re-layouts  1220 us
    unnamed x14, local copies, waits for them, and re-layouts  97.3 us
    add x6, other arithmetic, phi_blur(): phi_sum = phi_sum + weights[k][None, None, :] * padded[:, k:k + number, :]  86.5 us
    div x3, other arithmetic, body(): ratio = pixel_tiles / (blurred + 0.1)  65.5 us
    mul x3, other arithmetic, body(): estimate = estimate * chi_mix(ratio_sum, ratio_below, ratio_above)  64.1 us
    ppermute x12, starting transfers between devices, shifted(): return lax.ppermute(shard, axis, pairs)  36 us
  transfers between devices with their start and end apart: 13, of which 8 were waited for; matrix products, arithmetic and copies ran while one was open for 1% of the time, Pallas kernels for 0%

commit v1 on v0

--- a/solution.py
+++ b/solution.py
@@ -1,9 +1,22 @@
+import functools
 import jax
 import jax.numpy as jnp
 from jax import lax
 from jax.sharding import PartitionSpec as P
 
 ITERS = 3
+
+
+def _remake_series_all(u, on_dim, axis_k):
+    k_now = lax.axis_size("chi")
+    base_arr = jnp.split(u, k_now, axis=on_dim)
+    y_new = jnp.stack(base_arr, 0)
+    field_out = lax.all_to_all(y_new, axis_name="chi", split_axis=0, concat_axis=0)
+    carry_out = jnp.concatenate(field_out, axis_k)
+    return carry_out
+
+
+_write_roots = functools.partial(_remake_series_all, on_dim=2, axis_k=1)
 
 
 def shifted(shard, axis, by):
@@ -51,7 +64,7 @@
 
 def body(frames, drift_rows, drift_cols, weight_index, blur_band):
     corrected = jax.vmap(jax.vmap(shift_one))(frames, drift_rows, drift_cols, weight_index)
-    pixel_tiles = lax.all_to_all(corrected, "chi", split_axis=2, concat_axis=1, tiled=True)
+    pixel_tiles = _write_roots(corrected)
     weights = tap_weights(blur_band)
     estimate = pixel_tiles + 0.1
     for iteration in range(ITERS):

time: 1780 us -> 1610 us (0.904)
  local copies, waits for them, and re-layouts: 1420 us -> 1310 us
  other arithmetic: 254 us -> 191 us
    unnamed x14, local copies, waits for them, and re-layouts: 97.3 us -> 11.5 us
    all_to_all x3 -> x1, local copies, waits for them, and re-layouts: 30.9 us -> 4.62 us  [_remake_series_all(): lax.all_to_all(y_new, axis_name='chi', split_axis=0, concat_axis=0)]
    add x1 -> x0, local copies, waits for them, and re-layouts: 23.6 us -> none  [shift_one(): summed = summed + factor * window]
    add x6, other arithmetic: 86.5 us -> 63.9 us  [phi_blur(): phi_sum = phi_sum + weights[k][None, None, :] * padded[:, k:k + number, :]]
  transfers between devices with their start and end apart: 13 -> 13, of which waited for: 8 -> 8; matrix products, arithmetic and copies ran while one was open for 1% -> 2% of each run, Pallas kernels for 0% -> 0%
where the time goes in v1:
time: 1610 us; the launch traced here: 1580 us
  local copies, waits for them, and re-layouts  1310 us (81%)
  other arithmetic  191 us (12%)
  starting transfers between devices  41.6 us (3%)
  waiting for transfers between devices  34.3 us (2%)
    gather x768, local copies, waits for them, and re-layouts  1240 us
    add x6, other arithmetic, phi_blur(): phi_sum = phi_sum + weights[k][None, None, :] * padded[:, k:k + number, :]  63.9 us
    mul x3, other arithmetic, body(): estimate = estimate * chi_mix(ratio_sum, ratio_below, ratio_above)  53.4 us
    div x3, other arithmetic, body(): ratio = pixel_tiles / (blurred + 0.1)  52.7 us
    ppermute x12, starting transfers between devices, shifted(): return lax.ppermute(shard, axis, pairs)  35.8 us
  transfers between devices with their start and end apart: 13, of which 8 were waited for; matrix products, arithmetic and copies ran while one was open for 2% of the time, Pallas kernels for 0%

profile of v1, /device:TPU:30, one launch (start us, length us, event | category | flops | bytes accessed | tf_op | source)
XLA Modules:
  0.0 1582.2 jit_solution(16371779978393597203)
XLA Ops:
  0.9 8.4 pad_convert_fusion
  11.9 307.9 %while.4 = (s32[]{:T(128)}, f32[16,4,14,2098]{3,2,1,0:T(8,128)}, s32[64,4]{0,1:T(4,128)S(1)}, f32[64,8,2048]{2,1,0:T(8,128)}, s32[]{:T(128)}) while((s32[]{:T(128)}, f32[16,4,14,2098]{3,2,1,0:T(8,128)}, s32[64,4]{0,1:T(4,128)S(1)}, f32[64,8,2048]{2,1,0:T(8,128)}, s32[]{:T(128)}) %tuple.109), condition=%wide.while_cond, body=%wide.while_body.sunk | while | flops 2 | bytes 133761 | solution.py:38
  319.7 6.1 gather.21
  328.5 311.6 %while.5 = (s32[]{:T(128)}, f32[16,4,14,2098]{3,2,1,0:T(8,128)}, s32[64,4]{0,1:T(4,128)S(1)}, f32[64,8,2048]{2,1,0:T(8,128)}, s32[]{:T(128)}) while((s32[]{:T(128)}, f32[16,4,14,2098]{3,2,1,0:T(8,128)}, s32[64,4]{0,1:T(4,128)S(1)}, f32[64,8,2048]{2,1,0:T(8,128)}, s32[]{:T(128)}) %tuple.112), condition=%wide.while_cond.1, body=%wide.while_body.1.sunk | while | flops 2 | bytes 133761 | solution.py:38
  640.2 6.0 gather.23
  648.9 315.4 %while.6 = (s32[]{:T(128)}, f32[16,4,14,2098]{3,2,1,0:T(8,128)}, s32[64,4]{0,1:T(4,128)S(1)}, f32[64,8,2048]{2,1,0:T(8,128)}, s32[]{:T(128)}) while((s32[]{:T(128)}, f32[16,4,14,2098]{3,2,1,0:T(8,128)}, s32[64,4]{0,1:T(4,128)S(1)}, f32[64,8,2048]{2,1,0:T(8,128)}, s32[]{:T(128)}) %tuple.113), condition=%wide.while_cond.2, body=%wide.while_body.2.sunk | while | flops 2 | bytes 133761 | solution.py:38
  964.3 6.0 gather.25
  973.0 304.3 %while.7 = (s32[]{:T(128)}, f32[16,4,14,2098]{3,2,1,0:T(8,128)}, s32[64,4]{0,1:T(4,128)S(1)}, f32[64,8,2048]{2,1,0:T(8,128)}, s32[]{:T(128)}) while((s32[]{:T(128)}, f32[16,4,14,2098]{3,2,1,0:T(8,128)}, s32[64,4]{0,1:T(4,128)S(1)}, f32[64,8,2048]{2,1,0:T(8,128)}, s32[]{:T(128)}) %tuple.114), condition=%wide.while_cond.3, body=%wide.while_body.3.sunk | while | flops 2 | bytes 133761 | solution.py:38
  1277.3 6.1 gather.27
  1283.7 7.3 multiply_add_fusion
  1294.6 5.8 all-to-all-start
  1326.3 7.3 collective-permute-done.1
  1333.7 17.4 %fusion.99 = f32[16,8,8192]{2,0,1:T(8,128)} fusion(f32[15,8,8192]{2,0,1:T(8,128)} %get-tuple-element.108, f32[1,8,8192]{2,0,1:T(1,128)S(1)} %collective-permute-done, f32[1,8,8192]{2,0,1:T(1,128)S(1)} %collective-permute-done.1, f32[15,8,8192]{2,0,1:T(8,128)} %get-tuple-element.107, f32[2,16,4,8192]{3,1,2,0:T(8,128)} %copy-done, f32[8192]{0:T(1024)S(1)} %bitcast.115, ...), kind=kLoop, calls=%fused_computation.158 | loop fusion | flops 27262976 | bytes 21266432 | tf_op jit(solution)/shard_map/div | solution.py:75
  1351.1 12.1 fusion.24
  1378.8 17.8 %fusion.102 = f32[16,8,8192]{2,0,1:T(8,128)} fusion(f32[15,8,8192]{2,0,1:T(8,128)} %get-tuple-element.104, f32[1,8,8192]{2,0,1:T(1,128)S(1)} %collective-permute-done.2, f32[1,8,8192]{2,0,1:T(1,128)S(1)} %collective-permute-done.3, f32[15,8,8192]{2,0,1:T(8,128)} %get-tuple-element.103, f32[2,16,4,8192]{3,1,2,0:T(8,128)} %copy-done, f32[8192]{0:T(1024)S(1)} %bitcast.117, ...), kind=kLoop, calls=%fused_computation.163 | loop fusion | flops 27262976 | bytes 21266432 | tf_op jit(solution)/shard_map/mul | solution.py:79
  1396.6 12.1 fusion.40
  1423.5 17.6 %fusion.106 = f32[16,8,8192]{2,0,1:T(8,128)} fusion(f32[15,8,8192]{2,0,1:T(8,128)} %get-tuple-element.100, f32[1,8,8192]{2,0,1:T(1,128)S(1)} %collective-permute-done.4, f32[1,8,8192]{2,0,1:T(1,128)S(1)} %collective-permute-done.5, f32[15,8,8192]{2,0,1:T(8,128)} %get-tuple-element.99, f32[2,16,4,8192]{3,1,2,0:T(8,128)} %copy-done, f32[8192]{0:T(1024)S(1)} %bitcast.119, ...), kind=kLoop, calls=%fused_computation.169 | loop fusion | flops 27262976 | bytes 21266432 | tf_op jit(solution)/shard_map/div | solution.py:75
  1441.1 12.1 fusion.56
  1468.0 17.8 %fusion.109 = f32[16,8,8192]{2,0,1:T(8,128)} fusion(f32[16,8,8192]{2,0,1:T(8,128)} %fusion.102, f32[15,8,8192]{2,0,1:T(8,128)} %get-tuple-element.96, f32[1,8,8192]{2,0,1:T(1,128)S(1)} %collective-permute-done.6, f32[1,8,8192]{2,0,1:T(1,128)S(1)} %collective-permute-done.7, f32[15,8,8192]{2,0,1:T(8,128)} %get-tuple-element.95, f32[8192]{0:T(1024)S(1)} %bitcast.121, ...), kind=kLoop, calls=%fused_computation.174 | loop fusion | flops 26214400 | bytes 21266432 | tf_op jit(solution)/shard_map/mul | solution.py:79
  1485.9 12.1 fusion.72
  1513.0 17.6 %fusion.113 = f32[16,8,8192]{2,0,1:T(8,128)} fusion(f32[15,8,8192]{2,0,1:T(8,128)} %get-tuple-element.92, f32[1,8,8192]{2,0,1:T(1,128)S(1)} %collective-permute-done.8, f32[1,8,8192]{2,0,1:T(1,128)S(1)} %collective-permute-done.9, f32[15,8,8192]{2,0,1:T(8,128)} %get-tuple-element.91, f32[2,16,4,8192]{3,1,2,0:T(8,128)} %copy-done, f32[8192]{0:T(1024)S(1)} %bitcast.123, ...), kind=kLoop, calls=%fused_computation.180 | loop fusion | flops 27262976 | bytes 21266432 | tf_op jit(solution)/shard_map/div | solution.py:75
  1530.6 12.1 fusion.88
  1557.5 17.8 %fusion.116 = f32[16,8,8192]{2,0,1:T(8,128)} fusion(f32[16,8,8192]{2,0,1:T(8,128)} %fusion.109, f32[15,8,8192]{2,0,1:T(8,128)} %get-tuple-element.88, f32[1,8,8192]{2,0,1:T(1,128)S(1)} %collective-permute-done.10, f32[1,8,8192]{2,0,1:T(1,128)S(1)} %collective-permute-done.11, f32[15,8,8192]{2,0,1:T(8,128)} %get-tuple-element.87, f32[8192]{0:T(1024)S(1)} %bitcast.125, ...), kind=kLoop, calls=%fused_computation.185 | loop fusion | flops 26214400 | bytes 21266432 | tf_op jit(solution)/shard_map/mul | solution.py:79
  1575.4 6.6 copy.47
  (844 shorter events, 1355.1 us)
Async XLA Ops:
  1277.3 6.1 copy-start.3
  1294.6 10.3 all-to-all-start
  1309.5 2.0 copy-start
  1309.5 2.0 copy-start.2
  1311.5 4.2 copy-start.1
  1316.1 10.2 collective-permute-start
  1319.5 14.2 collective-permute-start.1
  1363.6 10.2 collective-permute-start.2
  1365.5 13.3 collective-permute-start.3
  1409.1 10.0 collective-permute-start.4
  1411.0 12.5 collective-permute-start.5
  1453.6 10.4 collective-permute-start.6
  1455.5 12.5 collective-permute-start.7
  1498.3 10.0 collective-permute-start.8
  1500.5 12.5 collective-permute-start.9
  1543.1 10.2 collective-permute-start.10
  1545.1 12.5 collective-permute-start.11
